TPU v7x, 32 devices: a whole 2x2x4 slice. The times are simulated.
32 devices in a mesh: dp: 8 (over y, x, core), mp: 4 (over z).
Axes of the slice: x: 2, y: 2, z: 4, core: 2. Of those that a mesh axis runs over, the one named last changes fastest.
Arguments:
- target_states: bfloat16 [1024, 4096], P('dp', 'mp')
- target_gain: float32 [4096], replicated, may hold values from 0.1 to 1.9
- target_head: bfloat16 [4096, 128256], P(None, ('dp', 'mp'))
- reference_states: bfloat16 [1024, 2048], P(('dp', 'mp'))
- reference_gain: float32 [2048], replicated, may hold values from 0.1 to 1.9
- reference_head: bfloat16 [2048, 128256], P(None, ('dp', 'mp'))
- token_ids: int32 [1024], P('dp'), may hold values from 0 to 128255
- reference_order: int32 [8], replicated, may hold values from 0 to 7, each once
Outputs:
- target_loss: float32 [1024], P('dp')
- reference_loss: float32 [1024], P('dp')
- reducible: float32 [8], P('dp')
Inputs may be any that keep to these rules, and one draw needn't show every extreme that they name: reference_states rows s * 128 to s * 128 + 127 belong to candidate sequence reference_order[s].
All inputs are finite; a program needn't handle non-finite values.
Results may differ from a plain program's by a relative error of at most 0.0041.
Values may be sent and summed in bfloat16 or wider, within the bound.
A program may use at most 128 MiB of HBM per device.

v0:
```python
import math

import jax
import jax.numpy as jnp
from jax import lax
from jax.sharding import PartitionSpec as P

LENGTH = 128


EPSILON = 1e-05


def normalize(states, gain):
    values = states.astype(jnp.float32)
    factor = lax.rsqrt(jnp.mean(values * values, axis=1, keepdims=True) + EPSILON)
    return (values * factor * gain[None, :]).astype(jnp.bfloat16)


def block_stats(logits, rows_id, columns):
    peak_val = jnp.max(logits, axis=1)
    exp_total = jnp.sum(jnp.exp(logits - peak_val[:, None]), axis=1)
    chosen = jnp.sum(jnp.where(columns[None, :] == rows_id[:, None], logits, 0.0), axis=1)
    return (peak_val, exp_total, chosen)


def shards(
    target_states,
    target_gain,
    target_head,
    reference_states,
    reference_gain,
    reference_head,
    token_ids,
    reference_order,
):
    vocab_width = target_head.shape[1]
    columns = lax.axis_index(("dp", "mp")) * vocab_width + jnp.arange(vocab_width, dtype=jnp.int32)
    rows_dp = target_states.shape[0]
    data_ways = lax.axis_size("dp")
    tokens = rows_dp * data_ways
    empty_float = jnp.zeros((tokens,), jnp.float32)
    empty_ids = jnp.zeros((tokens,), jnp.int32)
    gathered = lax.all_gather(target_states, "mp", axis=1, tiled=True)
    normed = normalize(gathered, target_gain)
    carry = (empty_float, empty_float, empty_float, empty_ids)
    start = jnp.int32(0)
    rows_x = lax.all_gather(normed, "dp", axis=0, tiled=True)
    rows_id = lax.all_gather(token_ids, "dp", axis=0, tiled=True)
    logits = jnp.dot(rows_x, target_head, preferred_element_type=jnp.float32)
    found = block_stats(logits, rows_id, columns) + (rows_id,)
    t_peak, t_total, t_pick, ids_all = tuple(
        (
            lax.dynamic_update_slice_in_dim(earlier, fresh_val, start, 0)
            for earlier, fresh_val in zip(carry, found)
        )
    )
    ref_normed = normalize(reference_states, reference_gain)
    ref_rows = lax.all_gather(ref_normed, ("dp", "mp"), axis=0, tiled=True)
    seq_count = tokens // LENGTH
    ref_ids = jnp.take(ids_all.reshape(seq_count, LENGTH), reference_order, axis=0).reshape(tokens)
    blocking = math.gcd(tokens, 512)

    def ref_block(packed):
        rows_x, rows_id = packed
        logits = jnp.dot(rows_x, reference_head, preferred_element_type=jnp.float32)
        return block_stats(logits, rows_id, columns)

    r_peak, r_total, r_pick = lax.map(
        ref_block,
        (ref_rows.reshape(-1, blocking, ref_rows.shape[1]), ref_ids.reshape(-1, blocking)),
    )
    r_peak = r_peak.reshape(tokens)
    r_total = r_total.reshape(tokens)
    r_pick = r_pick.reshape(tokens)
    t_max, r_max = lax.pmax((t_peak, r_peak), ("dp", "mp"))
    t_sum, t_hit, r_sum, r_hit = lax.psum(
        (t_total * jnp.exp(t_peak - t_max), t_pick, r_total * jnp.exp(r_peak - r_max), r_pick),
        ("dp", "mp"),
    )
    loss_target = t_max + jnp.log(t_sum) - t_hit
    loss_rows = r_max + jnp.log(r_sum) - r_hit
    matches = (reference_order[:, None] == jnp.arange(seq_count, dtype=jnp.int32)[None, :]).astype(
        jnp.float32
    )
    loss_reference = jnp.sum(
        matches[:, :, None] * loss_rows.reshape(seq_count, LENGTH)[:, None, :], axis=0
    ).reshape(tokens)
    first_row = lax.axis_index("dp") * rows_dp
    mine_target = lax.dynamic_slice_in_dim(loss_target, first_row, rows_dp, 0)
    mine_reference = lax.dynamic_slice_in_dim(loss_reference, first_row, rows_dp, 0)
    reducible = jnp.mean((mine_target - mine_reference).reshape(rows_dp // LENGTH, LENGTH), axis=1)
    return (mine_target, mine_reference, reducible)


def solution(mesh):
    placed = (
        P("dp", "mp"),
        P(),
        P(None, ("dp", "mp")),
        P(("dp", "mp"), None),
        P(),
        P(None, ("dp", "mp")),
        P("dp"),
        P(),
    )
    return jax.shard_map(
        shards, mesh=mesh, in_specs=placed, out_specs=(P("dp"), P("dp"), P("dp")), check_vma=False
    )
```

profile of v0, /device:TPU:0, one launch (start us, length us, event | category | flops | bytes accessed | tf_op | source)
XLA Modules:
  0.0 299.8 jit_solution(6555905454492770305)
XLA Ops:
  7.2 0.7 all-gather.5.cloned.1.call-update
  7.9 1.0 fusion.9
  9.0 1.7 fusion.11
  10.7 29.6 %all-gather.5.cloned.1.call-done = bf16[128,4096]{1,0:T(8,128)(2,1)} async-done(((bf16[128,1024]{1,0:T(8,128)(2,1)}), bf16[128,4096]{1,0:T(8,128)(2,1)}) %all-gather.5.cloned.1.call-update) | async-done | bytes 1048592 | tf_op jit(solution)/shard_map/all_gather | solution.py:44
  40.3 1.5 fusion.6
  41.8 2.6 fusion.8
  44.5 8.8 %all-gather = s32[8,1,128]{2,1,0:T(1,128)S(1)} all-gather(s32[1,1,128]{2,1,0:T(1,128)} %bitcast.56), channel_id=1, replica_groups=mesh['dp'=8,'mp'=4] {'dp'}, dimensions={0}, use_global_device_ids=true | all-gather | bytes 4608 | tf_op jit(solution)/shard_map/all_gather | solution.py:49
  53.3 0.7 compare_select_fusion
  54.0 0.6 gather_fusion
  54.5 0.7 compare_and_fusion
  55.2 0.1 broadcast_in_dim.48
  55.4 1.3 fusion.12
  56.7 47.6 %all-gather.9.cloned.1.call-done = bf16[1024,2048]{1,0:T(8,128)(2,1)} async-done(((bf16[32,2048]{1,0:T(8,128)(2,1)}), bf16[1024,2048]{1,0:T(8,128)(2,1)}) %all-gather.9.cloned.1.call-update) | async-done | bytes 4194320 | tf_op jit(solution)/shard_map/all_gather | solution.py:59
  104.3 41.7 %while.15 = (s32[]{:T(128)}, f32[2,512]{1,0:T(2,128)S(1)}, f32[2,512]{1,0:T(2,128)S(1)}, f32[2,512]{1,0:T(2,128)S(1)}, bf16[2,512,2048]{2,1,0:T(8,128)(2,1)}, /*...) while((s32[]{:T(128)}, f32[2,512]{1,0:T(2,128)S(1)}, ...), condition=%wide.region_12.13_spmd.clone, body=%wide.region_8.12_spmd.clone.sunk | while | flops 8417700352 | bytes 34989508 | solution.py:69
  104.3 14.8 %fusion.21 = (f32[512]{0:T(512)S(1)}, f32[512,4008]{0,1:T(8,128)}) fusion(bf16[2048,4008]{0,1:T(8,128)(2,1)} %get-tuple-element.186, bf16[2,512,2048]{2,1,0:T(8,128)(2,1)} %get-tuple-element.185, s32[]{:T(128)S(6)} %copy.24), kind=kOutput, calls=%fused_computation.38.clone.1 | convolution fusion | flops 8407436800 | bytes 26724356 | tf_op jit(solution)/shard_map/while/body/eval_jaxpr/dot_general | solution.py:66
  119.2 5.1 %select_reduce_fusion.3 = (f32[512]{0:T(512)S(1)}, f32[512]{0:T(512)S(1)}) fusion(f32[512,4008]{0,1:T(8,128)} %get-tuple-element.158, s32[512]{0:T(512)S(1)} %bitcast.47, s32[4008]{0:T(1024)S(1)} %iota_add_fusion.3, f32[512]{0:T(512)S(1)} %get-tuple-element.157), kind=kLoop, calls=%fused_computation.2.clone.1 | loop fusion | flops 10259456 | bytes 8232608 | tf_op jit(solution)/shard_map/while/body/eval_jaxpr/reduce_sum | solution.py:23
  124.4 16.3 %fusion.21 = (f32[512]{0:T(512)S(1)}, f32[512,4008]{0,1:T(8,128)}) fusion(bf16[2048,4008]{0,1:T(8,128)(2,1)} %get-tuple-element.186, bf16[2,512,2048]{2,1,0:T(8,128)(2,1)} %get-tuple-element.185, s32[]{:T(128)S(6)} %copy.24), kind=kOutput, calls=%fused_computation.38.clone.1 | convolution fusion | flops 8407436800 | bytes 26724356 | tf_op jit(solution)/shard_map/while/body/eval_jaxpr/dot_general | solution.py:66
  140.7 5.3 %select_reduce_fusion.3 = (f32[512]{0:T(512)S(1)}, f32[512]{0:T(512)S(1)}) fusion(f32[512,4008]{0,1:T(8,128)} %get-tuple-element.158, s32[512]{0:T(512)S(1)} %bitcast.47, s32[4008]{0:T(1024)S(1)} %iota_add_fusion.3, f32[512]{0:T(512)S(1)} %get-tuple-element.157), kind=kLoop, calls=%fused_computation.2.clone.1 | loop fusion | flops 10259456 | bytes 8232608 | tf_op jit(solution)/shard_map/while/body/eval_jaxpr/reduce_sum | solution.py:23
  146.1 13.2 %all-gather.7.cloned.1.call-done = bf16[1024,4096]{1,0:T(8,128)(2,1)} async-done(((bf16[128,4096]{1,0:T(8,128)(2,1)}), bf16[1024,4096]{1,0:T(8,128)(2,1)}) %all-gather.7.cloned.1.call-update) | async-done | bytes 8388624 | tf_op jit(solution)/shard_map/all_gather | solution.py:48
  159.3 42.1 %fusion.14 = (f32[1024]{0:T(1024)S(1)}, f32[1024,4008]{0,1:T(8,128)}) fusion(bf16[1024,4096]{1,0:T(8,128)(2,1)} %all-gather.7.cloned.1.call-done, bf16[4096,4008]{0,1:T(8,128)(2,1)} %param.12), kind=kOutput, calls=%fused_computation.39 | convolution fusion | flops 33625645056 | bytes 57643008 | tf_op jit(solution)/shard_map/dot_general | solution.py:50
  201.4 39.5 %all-reduce.1 = (f32[1024]{0:T(1024)S(1)}, f32[1024]{0:T(1024)S(1)}) all-reduce(f32[1024]{0:T(1024)S(1)} %get-tuple-element.100, f32[1024]{0:T(1024)S(1)} %bitcast.48), channel_id=1, replica_groups=mesh['dp'=8,'mp'=4] {'dp','mp'}, use_global_device_ids=true, to_apply=%region_2.0 | all-reduce | flops 2048 | bytes 16384 | tf_op jit(solution)/shard_map/pmax | solution.py:76
  240.9 8.0 %exponential_reduce_fusion.1 = (f32[1024]{0:T(1024)S(1)}, f32[1024]{0:T(1024)S(1)}) fusion(f32[1024,4008]{0,1:T(8,128)} %get-tuple-element.101, f32[1024]{0:T(1024)S(1)} %get-tuple-element.100, s32[1024]{0:T(1024)S(1)} %bitcast.43, s32[4008]{0:T(1024)S(1)} %iota_add_fusion.1), kind=kLoop, calls=%fused_computation.11 | loop fusion | flops 20518912 | bytes 16449184 | tf_op jit(solution)/shard_map/reduce_sum | solution.py:22
  248.9 41.2 %all-reduce = (f32[1024]{0:T(1024)S(1)}, f32[1024]{0:T(1024)S(1)}, f32[1024]{0:T(1024)S(1)}, f32[1024]{0:T(1024)S(1)}) all-reduce(f32[1024]{0:T(1024)S(1)} %get-tuple-element.72, f32[1024]{0:T(1024)S(1)} %get-tuple-element.103, f32[1024]{0:T(1024)S(1)} %bitcast.50, ...), channel_id=1, replica_groups=mesh['dp'=8,'mp'=4] {'dp','mp'}, use_global_device_ids=true, to_apply=%region_6.7 | all-reduce | flops 4096 | bytes 32768 | tf_op jit(solution)/shard_map/psum | solution.py:77
  290.3 1.2 subtract_reduce_fusion
  (34 shorter events, 0.7 us)
Async XLA Ops:
  7.2 33.1 %all-gather.5.cloned.1.call-start = ((), (), s32[]{:S(2)}) async-start(), calls=%async_computation | async-start | bytes 1310720 | tf_op jit(solution)/shard_map/all_gather | solution.py:44
  7.9 96.4 %all-gather.9.cloned.1.call-start = ((), (), s32[]{:S(2)}) async-start(), calls=%async_computation.2 | async-start | bytes 4325376 | tf_op jit(solution)/shard_map/all_gather | solution.py:59
  10.7 148.6 %all-gather.7.cloned.1.call-start = ((), (), s32[]{:S(2)}) async-start(), calls=%async_computation.1 | async-start | bytes 9437184 | tf_op jit(solution)/shard_map/all_gather | solution.py:48
  240.9 49.3 %copy-start = (f32[8,8]{1,0:T(8,128)S(1)}, f32[8,8]{1,0:T(8,128)}, u32[]{:S(2)}) copy-start(f32[8,8]{1,0:T(8,128)} %fusion.12) | copy-start | bytes 772
Sparse Core Ops, SparseCore 0:
  9.5 30.6 all-gather.4
  43.3 60.9 all-gather.8
  106.2 53.0 all-gather.6
where the time goes:
time: 300 us
  waiting for transfers between devices  91.1 us (30%)
  blocking collectives  89.6 us (30%)
  matrix products  73.2 us (24%)
  other arithmetic  29.1 us (10%)
  between operations  15.6 us (5%)
    all_gather x1, waiting for transfers between devices, shards(): ref_rows = lax.all_gather(ref_normed, ('dp', 'mp'), axis=0, tiled=True)  47.6 us
    dot_general x1, matrix products, shards(): logits = jnp.dot(rows_x, target_head, preferred_element_type=jnp.float32)  42.1 us
    psum x1, blocking collectives, shards(): lax.psum((t_total * jnp.exp(t_peak - t_max), t_pick, r_total * jnp.exp(r_...  41.2 us
    pmax x1, blocking collectives, shards(): t_max, r_max = lax.pmax((t_peak, r_peak), ('dp', 'mp'))  39.5 us
    dot_general x2, matrix products, ref_block(): logits = jnp.dot(rows_x, reference_head, preferred_element_type=jnp.float32)  31.1 us
    all_gather x1, waiting for transfers between devices, shards(): gathered = lax.all_gather(target_states, 'mp', axis=1, tiled=True)  29.6 us
    all_gather x1, waiting for transfers between devices, shards(): rows_x = lax.all_gather(normed, 'dp', axis=0, tiled=True)  13.2 us
    reduce_sum x2, other arithmetic, block_stats(): jnp.sum(jnp.where(columns[None, :] == rows_id[:, None], logits, 0.0), axi...  10.3 us
  transfers between devices with their start and end apart: 3, of which 3 were waited for; matrix products, arithmetic and copies ran while one was open for 17% of the time, Pallas kernels for 0%

commit v1 on v0

v1 whole, which is shorter than its diff:
```python
import functools

import jax
import jax.numpy as jnp
from jax import lax
from jax.experimental import pallas as pl
from jax.experimental.pallas import tpu as pltpu
from jax.sharding import PartitionSpec as P

EPSILON = 1e-05
MESH = pl.DeviceIdType.MESH
LANES = 128
FAR = 1 << 29
LEAST = -0.7 * 3.4e38


def flip(p, mask, bits):
    for j in range(bits):
        if (mask >> j) & 1:
            unit = 1 << j
            p = p + unit * (1 - 2 * ((p // unit) % 2))
    return p


def reverse(v, bits):
    return sum(((v >> j) & 1) << (bits - 1 - j) for j in range(bits))


def to_rows(column_block):
    return jnp.transpose(column_block)[0:8, :]


def to_column(row):
    return jnp.transpose(jnp.broadcast_to(row, (LANES, LANES)))


def kernel(
    cfg, order, inverse, ts, tg, rs, rg, ids8, th, rh, out,
    xt, xr, wfull, wlast, l0, l1, mx, sm, ht, idb, idall, ssend, sall, stat, sbuf, rbuf,
    send_sem, plane_sem, part_sem, ids_ssem, ids_rsem, ss_ssem, ss_rsem, fin_ssem, fin_rsem, wsem, lsem,
):
    dp, mp, planes, bits, chunk, tile, full, last = (
        cfg["dp"], cfg["mp"], cfg["planes"], cfg["bits"], cfg["chunk"], cfg["tile"], cfg["full"], cfg["last"]
    )
    half = tile // 2
    n = dp * mp
    d, z = lax.axis_index("dp"), lax.axis_index("mp")
    me = d * mp + z
    p, c = d // 2, d % 2
    other = 1 - c
    partner = (2 * p + other, z)
    rows, feats = ts.shape
    depth_t, depth_r = xt.shape[1], xr.shape[1]
    rrows = rs.shape[0]
    width = th.shape[1]
    base = me * width

    barrier = pltpu.get_barrier_semaphore()

    def greet(j, _):
        t = (me + j) % n
        pl.semaphore_signal(barrier, inc=1, device_id=(t // mp, t % mp), device_id_type=MESH)
        return 0

    lax.fori_loop(1, n, greet, 0)

    def blend(a, b):
        return a * (1 - c) + b * c

    def plane_of(v, core):
        a, b = flip(p, v, bits), flip(p, reverse(v, bits), bits)
        return a * (1 - core) + b * core

    def block(model, plane, core, zz):
        if model == 0:
            start = pl.multiple_of(((plane * 2 + core) * mp + zz) * rrows, rrows)
            return xr.at[pl.ds(start, rrows), :]
        start = pl.multiple_of((plane * 2 + core) * rows, rows)
        lane = pl.multiple_of(zz * feats, LANES)
        return xt.at[pl.ds(start, rows), pl.ds(lane, feats)]

    sent = []

    def push(model, ref, rsem, dev):
        pltpu.make_async_remote_copy(
            src_ref=ref, dst_ref=ref, send_sem=send_sem.at[len(sent)], recv_sem=rsem,
            device_id=dev, device_id_type=MESH,
        ).start()
        sent.append(model)

    def arrived(ref, rsem):
        pltpu.make_async_remote_copy(
            src_ref=ref, dst_ref=ref, send_sem=send_sem.at[0], recv_sem=rsem,
            device_id=partner, device_id_type=MESH,
        ).wait_recv()

    def slot(model, v, i):
        return (model * planes + v) * mp + i

    def event(model, v, i):
        zz = (z + i) % mp
        ref = block(model, plane_of(v, c), c, zz)
        if (v, i) != (0, 0):
            arrived(ref, plane_sem.at[slot(model, v, i)])
        else:
            for k in range(1, mp):
                push(model, ref, plane_sem.at[slot(model, 0, mp - k)], (d, (z + k) % mp))
        high = v.bit_length()
        for k in range(high, bits):
            near = blend(flip(p, 1 << k, bits), flip(p, 1 << (bits - 1 - k), bits))
            push(model, ref, plane_sem.at[slot(model, v | (1 << k), i)], (2 * near + c, z))
        push(model, ref, part_sem.at[slot(model, v, i)], partner)

    def partner_ready(model, r):
        v = r * (1 - other) + reverse(r, bits) * other
        plane = flip(p, r, bits)
        for i in range(mp):
            arrived(block(model, plane, other, (z + i) % mp), part_sem.at[(model * planes + v) * mp + i])

    models = [0] * (planes // 2) + [1] * (planes // 2)

    def full_copy(model, i, s):
        head, depth = (rh, depth_r) if model == 0 else (th, depth_t)
        return pltpu.make_async_copy(
            head.at[:, pl.ds(pl.multiple_of(i * tile, LANES), tile)], wfull.at[s, pl.ds(0, depth), :], wsem.at[s]
        )

    def last_copy(model):
        head, depth = (rh, depth_r) if model == 0 else (th, depth_t)
        return pltpu.make_async_copy(
            head.at[:, pl.ds(full * tile, last)], wlast.at[pl.ds(0, depth), :], lsem.at[0]
        )

    full_copy(0, 0, 0).start()
    last_copy(0).start()

    values = ts[...].astype(jnp.float32)
    mine = jnp.sum(values * values, axis=1, keepdims=True)
    ssend[...] = to_rows(jnp.broadcast_to(mine, (rows, LANES)))
    rvals = rs[...].astype(jnp.float32)
    rfac = lax.rsqrt(jnp.sum(rvals * rvals, axis=1, keepdims=True) / depth_r + EPSILON)
    own_r = pl.multiple_of(me * rrows, rrows)
    xr[pl.ds(own_r, rrows), :] = (rvals * rfac * rg[...]).astype(jnp.bfloat16)
    idall[d] = ids8[...]

    pl.semaphore_wait(barrier, n - 1)

    small = []
    for k in range(1, mp):
        cp = pltpu.make_async_remote_copy(
            src_ref=ssend, dst_ref=sall.at[mp - k], send_sem=ss_ssem.at[k], recv_sem=ss_rsem.at[mp - k],
            device_id=(d, (z + k) % mp), device_id_type=MESH,
        )
        cp.start()
        small.append(cp)
    event(0, 0, 0)
    for k in range(1, dp):
        cp = pltpu.make_async_remote_copy(
            src_ref=ids8, dst_ref=idall.at[d], send_sem=ids_ssem.at[k], recv_sem=ids_rsem.at[dp - k],
            device_id=((d + k) % dp, z), device_id_type=MESH,
        )
        cp.start()
        small.append(cp)

    total = ssend[...]
    for k in range(1, mp):
        pltpu.make_async_remote_copy(
            src_ref=ssend, dst_ref=sall.at[k], send_sem=ss_ssem.at[k], recv_sem=ss_rsem.at[k],
            device_id=partner, device_id_type=MESH,
        ).wait_recv()
        total = total + sall[k]
    factor = to_column(lax.rsqrt(total / depth_t + EPSILON)[0:1, :])
    for g in range(feats // LANES):
        at = pl.multiple_of(z * feats + g * LANES, LANES)
        part = ts[:, g * LANES : (g + 1) * LANES].astype(jnp.float32)
        xt[pl.ds(pl.multiple_of(d * rows, rows), rows), pl.ds(at, LANES)] = (
            part * factor * tg[:, pl.ds(at, LANES)]
        ).astype(jnp.bfloat16)

    for i in range(1, mp):
        event(0, 0, i)
    event(1, 0, 0)

    for k in range(1, dp):
        src = (d + k) % dp
        pltpu.make_async_remote_copy(
            src_ref=ids8, dst_ref=idall.at[src], send_sem=ids_ssem.at[k], recv_sem=ids_rsem.at[k],
            device_id=partner, device_id_type=MESH,
        ).wait_recv()

    vs = sorted(range(planes), key=lambda v: (bin(v).count("1"), v))

    def needed(a):
        want = [2 * a, 2 * a + 1, reverse(2 * a, bits), reverse(2 * a + 1, bits)]
        return max(vs.index(v) for v in want) + 1

    count = planes // 2
    todo = {0: [(0, v, i) for v in vs[1:] for i in range(mp)], 1: [(1, v, i) for v in vs for i in range(mp)][1:]}

    def flush(model, a):
        keep = set(vs[: needed(a)])
        while any(v in keep for _, v, _ in todo[model]):
            event(*todo[model].pop(0))

    lane = lax.broadcasted_iota(jnp.int32, (1, LANES), 1)
    strip = 64

    def stats(buf, offset, wide):
        groups = -(-wide // LANES)
        for r in range(0, chunk, strip):
            at = pl.ds(r, strip)
            m_old = mx[at, :]
            pieces = []
            for g in range(groups):
                piece = buf[at, g * LANES : (g + 1) * LANES]
                if (g + 1) * LANES > wide:
                    piece = jnp.where(lane < wide - g * LANES, piece, LEAST)
                pieces.append(piece)
            m_new = functools.reduce(jnp.maximum, pieces, m_old)
            rel = idb[at, :] - offset
            tot = sm[at, :] * jnp.exp(m_old - m_new)
            hit = ht[at, :]
            for g in range(groups):
                tot = tot + jnp.exp(pieces[g] - m_new)
                match = rel == lane + g * LANES
                if (g + 1) * LANES > wide:
                    match = match & (lane < wide - g * LANES)
                hit = hit + jnp.where(match, pieces[g], 0.0)
            mx[at, :] = m_new
            sm[at, :] = tot
            ht[at, :] = hit

    step = 0
    for index, model in enumerate(models):
        a = index % count
        x, depth = (xr, depth_r) if model == 0 else (xt, depth_t)
        flush(model, a)
        for r in (2 * a, 2 * a + 1):
            partner_ready(model, r)
        plane = flip(p, 2 * a, bits)
        first = (plane // 2) * 2
        start = pl.multiple_of(first * 2 * rows, chunk)
        for s in range(chunk // LANES):
            which = first * 2 + s
            src = order[which] if model == 0 else which
            idb[s * LANES : (s + 1) * LANES, :] = to_column(idall[src][0:1, :]) - base
        mx[...] = jnp.full(mx.shape, LEAST, jnp.float32)
        sm[...] = jnp.zeros(sm.shape, jnp.float32)
        ht[...] = jnp.zeros(ht.shape, jnp.float32)
        l1[...] = jnp.full(l1.shape, LEAST, jnp.float32)

        if model == 0 and a + 1 < count:
            ahead = todo[0] + todo[1][: mp - 1]
            todo[1] = todo[1][mp - 1 :]
            todo[0] = []
        elif model == 0:
            keep = set(vs[: needed(0)])
            ahead = [e for e in todo[1] if e[1] in keep]
            todo[1] = todo[1][len(ahead) :]
        else:
            ahead, todo[1] = todo[1], []
        if index > 0:
            last_copy(model).start()
        upcoming = models[index + 1] if index + 1 < len(models) else None
        at_step = {}
        for e, item in enumerate(ahead):
            at_step.setdefault(e * full // max(len(ahead), 1), []).append(item)

        def body(i, _, model=model, x=x, depth=depth, start=start, step=step, upcoming=upcoming, at_step=at_step):
            s = (step + i) % 2
            full_copy(model, i, s).wait()

            @pl.when(i + 1 < full)
            def _():
                full_copy(model, i + 1, 1 - s).start()

            if upcoming is not None:
                @pl.when(i + 1 == full)
                def _():
                    full_copy(upcoming, 0, 1 - s).start()

            for when, items in at_step.items():
                @pl.when(i == when)
                def _():
                    for item in items:
                        event(*item)

            lhs = x.at[pl.ds(start, chunk), :]
            l0[...] = jnp.dot(lhs[...], wfull[s, 0:depth, 0:half], preferred_element_type=jnp.float32)
            stats(l1, jnp.where(i == 0, FAR, i * tile - half), half)
            l1[...] = jnp.dot(lhs[...], wfull[s, 0:depth, half:tile], preferred_element_type=jnp.float32)
            stats(l0, i * tile, half)
            return 0

        lax.fori_loop(0, full, body, 0)
        step += full
        lhs = x.at[pl.ds(start, chunk), :]
        last_copy(model).wait()
        l0[...] = jnp.dot(lhs[...], wlast[0:depth, 0:half], preferred_element_type=jnp.float32)
        stats(l1, full * tile - half, half)
        l1[:, 0 : last - half] = jnp.dot(lhs[...], wlast[0:depth, half:last], preferred_element_type=jnp.float32)
        stats(l0, full * tile, half)
        stats(l1, full * tile + half, last - half)
        for s in range(chunk // LANES):
            at = pl.ds(s * LANES, LANES)
            top = jnp.max(mx[at, :], axis=1, keepdims=True)
            tot = jnp.sum(sm[at, :] * jnp.exp(mx[at, :] - top), axis=1, keepdims=True)
            hit = jnp.sum(ht[at, :], axis=1, keepdims=True)
            mixed = jnp.where(lane == 0, top, jnp.where(lane == 1, tot, hit))
            stat[model, first * 2 + s] = to_rows(mixed)

    for k in range(dp):
        sbuf[k, 0:8, :] = stat[1, k]
        sbuf[k, 8:16, :] = stat[0, inverse[k]]

    def deliver(k):
        t = (me + k) % n
        return pltpu.make_async_remote_copy(
            src_ref=sbuf.at[t // mp], dst_ref=rbuf.at[n - k], send_sem=fin_ssem.at[k], recv_sem=fin_rsem.at[n - k],
            device_id=(t // mp, t % mp), device_id_type=MESH,
        )

    def start_one(k, _):
        deliver(k).start()
        return 0

    lax.fori_loop(1, n, start_one, 0)
    rbuf[0] = sbuf[d]
    for k, model in enumerate(sent):
        ref = block(model, p, c, z)
        pltpu.make_async_remote_copy(
            src_ref=ref, dst_ref=ref, send_sem=send_sem.at[k], recv_sem=plane_sem.at[0],
            device_id=partner, device_id_type=MESH,
        ).wait_send()
    for copy in small:
        copy.wait_send()

    def wait_one(k, _):
        deliver(k).wait()
        return 0

    lax.fori_loop(1, n, wait_one, 0)

    parts = []
    for off in (0, 8):
        top = rbuf[0, off : off + 1, :]
        for k in range(1, n):
            top = jnp.maximum(top, rbuf[k, off : off + 1, :])
        tot = jnp.zeros_like(top)
        hit = jnp.zeros_like(top)
        for k in range(n):
            tot = tot + rbuf[k, off + 1 : off + 2, :] * jnp.exp(rbuf[k, off : off + 1, :] - top)
            hit = hit + rbuf[k, off + 2 : off + 3, :]
        parts.append(top + jnp.log(tot) - hit)
    loss_t, loss_r = parts
    mean = jnp.sum(loss_t - loss_r, axis=1, keepdims=True) / rows
    out[0:1, :] = loss_t
    out[1:2, :] = loss_r
    out[2:3, :] = jnp.broadcast_to(mean, (1, LANES))
    out[3:8, :] = jnp.zeros((5, LANES), jnp.float32)


def shards(dp, mp, ts, tg, th, rs, rg, rh, ids, order):
    rows, feats = ts.shape
    width = th.shape[1]
    depth_t, depth_r = th.shape[0], rh.shape[0]
    tokens = rows * dp
    planes = dp // 2
    bits = planes.bit_length() - 1
    chunk = 4 * rows
    tile = 512
    full = (width - 1) // tile
    last = width - full * tile
    cfg = dict(dp=dp, mp=mp, planes=planes, bits=bits, chunk=chunk, tile=tile, full=full, last=last)
    n = dp * mp
    seqs = order.shape[0]
    inverse = jnp.sum(
        jnp.where(order[:, None] == jnp.arange(seqs, dtype=jnp.int32)[None, :],
                  jnp.arange(seqs, dtype=jnp.int32)[:, None], 0), axis=0).astype(jnp.int32)
    ids8 = jnp.broadcast_to(ids[None, :], (8, rows))
    hops = sum(bits - v.bit_length() + 1 for v in range(planes)) * mp + mp - 1
    f32 = jnp.float32
    vmem = pl.BlockSpec(memory_space=pltpu.VMEM)
    smem = pl.BlockSpec(memory_space=pltpu.SMEM)
    anyspace = pl.BlockSpec(memory_space=pl.ANY)
    dma = pltpu.SemaphoreType.DMA
    out = pl.pallas_call(
        functools.partial(kernel, cfg),
        out_shape=jax.ShapeDtypeStruct((8, LANES), f32),
        in_specs=[smem, smem, vmem, vmem, vmem, vmem, vmem, anyspace, anyspace],
        out_specs=vmem,
        scratch_shapes=[
            pltpu.VMEM((tokens, depth_t), jnp.bfloat16),
            pltpu.VMEM((tokens, depth_r), jnp.bfloat16),
            pltpu.VMEM((2, depth_t, tile), jnp.bfloat16),
            pltpu.VMEM((depth_t, last), jnp.bfloat16),
            pltpu.VMEM((chunk, tile // 2), f32),
            pltpu.VMEM((chunk, tile // 2), f32),
            pltpu.VMEM((chunk, LANES), f32),
            pltpu.VMEM((chunk, LANES), f32),
            pltpu.VMEM((chunk, LANES), f32),
            pltpu.VMEM((chunk, LANES), jnp.int32),
            pltpu.VMEM((dp, 8, rows), jnp.int32),
            pltpu.VMEM((8, LANES), f32),
            pltpu.VMEM((mp, 8, LANES), f32),
            pltpu.VMEM((2, dp, 8, LANES), f32),
            pltpu.VMEM((dp, 16, LANES), f32),
            pltpu.VMEM((n, 16, LANES), f32),
            dma((2 * hops,)),
            dma((2 * planes * mp,)),
            dma((2 * planes * mp,)),
            dma((dp,)),
            dma((dp,)),
            dma((mp,)),
            dma((mp,)),
            dma((n,)),
            dma((n,)),
            dma((2,)),
            dma((1,)),
        ],
        compiler_params=pltpu.CompilerParams(
            collective_id=0, has_side_effects=True, vmem_limit_bytes=60 * 1024 * 1024
        ),
    )(order, inverse, ts, tg[None, :], rs, rg[None, :], ids8, th, rh)
    return out[0], out[1], out[2, 0 : rows // LANES]


def solution(mesh):
    placed = (
        P("dp", "mp"),
        P(),
        P(None, ("dp", "mp")),
        P(("dp", "mp"), None),
        P(),
        P(None, ("dp", "mp")),
        P("dp"),
        P(),
    )
    return jax.shard_map(
        functools.partial(shards, mesh.shape["dp"], mesh.shape["mp"]),
        mesh=mesh, in_specs=placed, out_specs=(P("dp"), P("dp"), P("dp")), check_vma=False,
    )
```

time: 300 us -> 194 us (0.65)
  Pallas kernels: 0 us -> 124 us
  waiting for transfers between devices: 91.1 us -> 0 us
  blocking collectives: 89.6 us -> 0 us
  matrix products: 73.2 us -> 0 us
  local copies, waits for them, and re-layouts: 0.99 us -> 65.8 us
  other arithmetic: 29.1 us -> 1.25 us
  between operations: 15.6 us -> 0.64 us
    pallas_call x0 -> x1, Pallas kernels: none -> 124 us  [shards(): pl.pallas_call(functools.partial(kernel, cfg), out_shape=jax.ShapeDtypeSt...]
    all_gather x3 -> x0, waiting for transfers between devices: 90.4 us -> none  [the longest x1 47.6 us: shards(): ref_rows = lax.all_gather(ref_normed, ('dp', 'mp'), axis=0, tiled=True)]
    dot_general x3 -> x0, matrix products: 73.2 us -> none  [the longest x1 42.1 us: shards(): logits = jnp.dot(rows_x, target_head, preferred_element_type=jnp.float32)]
    unnamed x6 -> x2, local copies, waits for them, and re-layouts: 0.09 us -> 62.1 us
    psum x1 -> x0, blocking collectives: 41.2 us -> none  [shards(): lax.psum((t_total * jnp.exp(t_peak - t_max), t_pick, r_total * jnp.exp(r_...]
    pmax x1 -> x0, blocking collectives: 39.5 us -> none  [shards(): t_max, r_max = lax.pmax((t_peak, r_peak), ('dp', 'mp'))]
    reduce_sum x7 -> x1, other arithmetic: 22.1 us -> 1.25 us  [shards(): jnp.sum(jnp.where(order[:, None] == jnp.arange(seqs, dtype=jnp.int32)[Non...]
    all_gather x1 -> x0, blocking collectives: 8.85 us -> none  [shards(): rows_id = lax.all_gather(token_ids, 'dp', axis=0, tiled=True)]
  transfers between devices with their start and end apart: 3 -> 0, of which waited for: 3 -> 0; matrix products, arithmetic and copies ran while one was open for 17% -> 0% of each run, Pallas kernels for 0% -> 0%
where the time goes in v1:
time: 194 us; the launch traced here: 192 us
  Pallas kernels  124 us (64%)
  local copies, waits for them, and re-layouts  65.8 us (34%)
    pallas_call x1, Pallas kernels, shards(): pl.pallas_call(functools.partial(kernel, cfg), out_shape=jax.ShapeDtypeSt...  124 us
    unnamed x2, local copies, waits for them, and re-layouts  62.1 us

profile of v1, /device:TPU:0, one launch (start us, length us, event | category | flops | bytes accessed | tf_op | source)
XLA Modules:
  0.0 191.7 jit_solution(8080966216780389780)
XLA Ops:
  0.6 1.2 select_reduce_fusion.inverse
  1.9 1.2 broadcast_in_dim.31.ids8
  3.1 20.8 %copy.14.rh = bf16[2048,4008]{1,0:T(8,128)(2,1)} copy(bf16[2048,4008]{0,1:T(8,128)(2,1)} %param.13) | data formatting | bytes 32833536 | tf_op args[5]
  24.0 41.3 %copy.13.th = bf16[4096,4008]{1,0:T(8,128)(2,1)} copy(bf16[4096,4008]{0,1:T(8,128)(2,1)} %param.10) | data formatting | bytes 65667072 | tf_op args[2]
  65.2 124.0 %shard_map.103 = f32[8,128]{1,0:T(8,128)} custom-call(s32[8]{0:T(128)} %order.1, s32[8]{0:T(128)} %select_reduce_fusion.inverse, bf16[128,1024]{1,0:T(8,128)(2,1)} %ts.1, f32[1,4096]{1,0:T(1,128)} %bitcast.7, bf16[32,2048]{1,0:T(8,128)(2,1)} %rs.1, f32[1,2048]{1,0:T(1,128)} %bitcast.8, s32[8,128]{1,0:T(8,128)} %broadcast_in_dim.31.ids8, ...), custom_call_target="tpu_custom_call" | custom-call | tf_op jit(solution)/shard_map/pallas_call | solution.py:387
  189.2 1.2 slice.11
  190.4 1.3 slice_bitcast_fusion
